TPU v7x, 256 devices: a whole 4x4x8 slice. The times are simulated.
256 devices in a mesh: grp: 32 (over x, y, core), tp: 8 (over z).
Axes of the slice: x: 4, y: 4, z: 8, core: 2. Of those that a mesh axis runs over, the one named last changes fastest.
Arguments:
- hidden_in: bfloat16 [512, 2048], P('grp'), may hold values from -6 to 6
- norm_gain: bfloat16 [2048], replicated, may hold values from 0.099609375 to 1.8984375
- w_query: bfloat16 [2048, 2048], P(None, 'tp'), may hold values from -0.125 to 0.125
- w_keyval: bfloat16 [2048, 512], P(None, 'tp'), may hold values from -0.125 to 0.125
- w_output: bfloat16 [2048, 2048], P('tp'), may hold values from -0.125 to 0.125
- prefix_cache: bfloat16 [64, 512, 512], P('grp', 'tp'), may hold values from -130 to 130
- private_cache: bfloat16 [512, 512, 512], P('grp', 'tp'), may hold values from -130 to 130
- node_parent: int32 [64], replicated, may hold values from 0 to 3, as said below
- node_length: int32 [64], replicated, may hold values from 1 to 512, as said below
- request_node: int32 [512], replicated, may hold values from 4 to 63, as said below
- private_length: int32 [512], P('grp'), may hold values from 0 to 512, as said below
Outputs:
- hidden_out: bfloat16 [512, 2048], P('grp', 'tp')
- new_keyval: bfloat16 [512, 512], P('grp', 'tp')
Inputs may be any that keep to these rules, and one draw needn't show every extreme that they name: `node_parent`: nodes 0 to 3 are the tenants' roots and are their own parents; every other node's parent is a root, and every root has a child. `request_node`: request r belongs to tenant r // 128; its node is a non-root node whose parent is that tenant's root. `node_length`: the longest node has exactly 512 used slots. `private_length`: some request has exactly 512 used slots.
All inputs are finite; a program needn't handle non-finite values.
Results may differ from a plain program's by a relative error of at most 0.023.
Values may be sent and summed in bfloat16 or wider, within the bound.
A program may use at most 128 MiB of HBM per device.

v0:
```python
import math
import jax
import jax.numpy as jnp
from jax import lax
from jax.sharding import PartitionSpec as P

HEADS = 32
KV_HEADS = 4
HEAD_DIM = 64
TENANTS = 4


def combined_all(x, axis, combine):
    everything = jax.tree.map(
        lambda part, kind: lax.all_gather(part.astype(kind), axis),
        x,
        (jnp.bfloat16, jnp.bfloat16, jnp.bfloat16),
    )

    def take(k):
        return jax.tree.map(lambda part, own: part[k].astype(own.dtype), everything, x)

    return lax.fori_loop(
        1, lax.axis_size(axis), lambda k, so_far: combine(so_far, take(k)), take(0)
    )


def rms_norm(values, scale_gain):
    floats = values.astype(jnp.float32)
    spread = jnp.mean(floats * floats, axis=-1, keepdims=True)
    return (floats * lax.rsqrt(spread + 1e-05) * scale_gain.astype(jnp.float32)).astype(
        jnp.bfloat16
    )


def rotate(head_rows, position):
    half_dim = head_rows.shape[-1] // 2
    freq_index = jnp.arange(half_dim, dtype=jnp.float32)
    frequency = jnp.exp(freq_index * (-2.0 * math.log(10000.0) / head_rows.shape[-1]))
    angles = position[:, None, None] * frequency[None, None, :]
    cosine = jnp.cos(angles)
    sine_part = jnp.sin(angles)
    front_half = head_rows[..., :half_dim]
    back_half = head_rows[..., half_dim:]
    return jnp.concatenate(
        [front_half * cosine - back_half * sine_part, back_half * cosine + front_half * sine_part],
        axis=-1,
    )


def softmax_part(queries, key_rows, value_rows, valid, shared):
    row_count = queries.shape[0]
    grouped = queries.reshape(row_count, KV_HEADS, HEADS // KV_HEADS, HEAD_DIM)
    if shared:
        scores = jnp.einsum("nkgd,lkd->nkgl", grouped, key_rows, preferred_element_type=jnp.float32)
    else:
        scores = jnp.einsum(
            "nkgd,nlkd->nkgl", grouped, key_rows, preferred_element_type=jnp.float32
        )
    scores = scores * HEAD_DIM ** (-0.5)
    usable = valid[:, None, None, :]
    scores = jnp.where(usable, scores, -jnp.inf)
    maxima = jnp.maximum(jnp.max(scores, axis=-1), -1e30)
    weights = jnp.where(usable, jnp.exp(scores - maxima[..., None]), 0.0)
    totals = jnp.sum(weights, axis=-1)
    rounded = weights.astype(jnp.bfloat16)
    if shared:
        weighted = jnp.einsum(
            "nkgl,lkd->nkgd", rounded, value_rows, preferred_element_type=jnp.float32
        )
    else:
        weighted = jnp.einsum(
            "nkgl,nlkd->nkgd", rounded, value_rows, preferred_element_type=jnp.float32
        )
    return (weighted, maxima, totals)


def merge_pair(left_part, right_part):
    left_sum, left_max, left_total = left_part
    right_sum, right_max, right_total = right_part
    upper = jnp.maximum(left_max, right_max)
    left_factor = jnp.exp(left_max - upper)
    right_factor = jnp.exp(right_max - upper)
    merged_sum = left_sum * left_factor[..., None] + right_sum * right_factor[..., None]
    return (merged_sum, upper, left_total * left_factor + right_total * right_factor)


def add_token(weighted, maxima, totals, token_score, token_value, form):
    upper = jnp.maximum(maxima, token_score)
    former = jnp.exp(maxima - upper)
    fresh = jnp.exp(token_score - upper)
    summed = weighted * former[..., None] + jnp.einsum(
        form, fresh.astype(jnp.bfloat16), token_value, preferred_element_type=jnp.float32
    )
    return summed / (totals * former + fresh)[..., None]


def on_device(
    hidden_in,
    norm_gain,
    w_query,
    w_keyval,
    w_output,
    prefix_cache,
    private_cache,
    node_parent,
    node_length,
    request_node,
    private_length,
):
    grp_index = lax.axis_index("grp")
    tp_index = lax.axis_index("tp")
    req_dev = hidden_in.shape[0]
    total_req = request_node.shape[0]
    per_tenant = total_req // TENANTS
    share_count = HEADS // KV_HEADS
    key_width = KV_HEADS * HEAD_DIM
    local_heads = w_query.shape[1] // HEAD_DIM
    local_kv = w_keyval.shape[1] // HEAD_DIM
    slice_width = local_heads * HEAD_DIM
    node_dev = prefix_cache.shape[0]
    local_len = prefix_cache.shape[1]
    priv_len = private_cache.shape[1]
    scale_factor = HEAD_DIM ** (-0.5)
    normed = rms_norm(hidden_in, norm_gain)
    query = jnp.dot(normed, w_query, preferred_element_type=jnp.float32)
    keyval = jnp.dot(normed, w_keyval, preferred_element_type=jnp.float32)
    own_mid = lax.dynamic_slice_in_dim(request_node, grp_index * req_dev, req_dev)
    own_root = node_parent[own_mid]
    position = (node_length[own_root] + node_length[own_mid] + private_length).astype(jnp.float32)
    query_rot = (
        rotate(query.reshape(req_dev, local_heads, HEAD_DIM), position)
        .reshape(req_dev, slice_width)
        .astype(jnp.bfloat16)
    )
    kv_rows = keyval.reshape(req_dev, local_kv, HEAD_DIM)
    is_key = tp_index * local_kv + jnp.arange(local_kv) < KV_HEADS
    new_keyval = (
        jnp.where(is_key[None, :, None], rotate(kv_rows, position), kv_rows)
        .reshape(req_dev, local_kv * HEAD_DIM)
        .astype(jnp.bfloat16)
    )
    query_all, keyval_all = (
        lax.all_gather(query_rot, "tp", axis=1, tiled=True),
        lax.all_gather(new_keyval, "tp", axis=1, tiled=True),
    )
    everyone = lax.all_gather(query_all, "grp", axis=0, tiled=True)
    private_valid = (tp_index * priv_len + jnp.arange(priv_len))[None, :] < private_length[:, None]
    private_keys = private_cache[:, :, :key_width].reshape(req_dev, priv_len, KV_HEADS, HEAD_DIM)
    private_values = private_cache[:, :, key_width:].reshape(req_dev, priv_len, KV_HEADS, HEAD_DIM)
    private_part = softmax_part(query_all, private_keys, private_values, private_valid, False)
    slot_positions = tp_index * local_len + jnp.arange(local_len)
    node_parts = []
    for node_slot in range(node_dev):
        node_id = grp_index * node_dev + node_slot
        is_root = node_id < TENANTS
        member = jnp.where(is_root, node_parent[request_node] == node_id, request_node == node_id)
        order_key = jnp.where(member, 0, total_req) + jnp.arange(total_req)
        picked = lax.top_k(-order_key, per_tenant)[1]
        filled = jnp.arange(per_tenant) < jnp.sum(member.astype(jnp.int32))
        chosen = jnp.take(everyone, picked, axis=0)
        node_rows = prefix_cache[node_slot]
        node_keys = node_rows[:, :key_width].reshape(local_len, KV_HEADS, HEAD_DIM)
        node_values = node_rows[:, key_width:].reshape(local_len, KV_HEADS, HEAD_DIM)
        node_valid = (slot_positions < node_length[node_id])[None, :]
        weighted, maxima, totals = softmax_part(chosen, node_keys, node_values, node_valid, True)
        level_slot = jnp.where(is_root, 0, 1)
        node_parts.append((picked, filled, level_slot, weighted, maxima, totals))
    sum_rows = jnp.zeros((total_req, 2, HEADS * HEAD_DIM), jnp.float32)
    max_rows = jnp.zeros((total_req, 2, HEADS), jnp.float32)
    total_rows = jnp.zeros((total_req, 2, HEADS), jnp.float32)
    for entry in node_parts:
        picked, filled, level_slot, weighted, maxima, totals = entry
        keep = filled[:, None]
        sum_rows = sum_rows.at[picked, level_slot].add(
            jnp.where(keep, weighted.reshape(per_tenant, HEADS * HEAD_DIM), 0.0)
        )
        max_rows = max_rows.at[picked, level_slot].add(
            jnp.where(keep, maxima.reshape(per_tenant, HEADS), 0.0)
        )
        total_rows = total_rows.at[picked, level_slot].add(
            jnp.where(keep, totals.reshape(per_tenant, HEADS), 0.0)
        )
    back_sum, back_max, back_total = (
        lax.psum_scatter(sum_rows, "grp", scatter_dimension=0, tiled=True),
        lax.psum_scatter(max_rows, "grp", scatter_dimension=0, tiled=True),
        lax.psum_scatter(total_rows, "grp", scatter_dimension=0, tiled=True),
    )
    stat_shape = (req_dev, 2, KV_HEADS, share_count)
    back_sum = back_sum.reshape(req_dev, 2, KV_HEADS, share_count, HEAD_DIM)
    back_max = back_max.reshape(stat_shape)
    back_total = back_total.reshape(stat_shape)
    root_part = (back_sum[:, 0], back_max[:, 0], back_total[:, 0])
    mid_part = (back_sum[:, 1], back_max[:, 1], back_total[:, 1])
    local_sum, local_max, local_total = merge_pair(merge_pair(root_part, mid_part), private_part)
    full_sum, full_max, full_total = combined_all(
        (local_sum, local_max, local_total), "tp", merge_pair
    )
    grouped = query_all.reshape(req_dev, KV_HEADS, share_count, HEAD_DIM)
    token_keys = keyval_all[:, :key_width].reshape(req_dev, KV_HEADS, HEAD_DIM)
    token_values = keyval_all[:, key_width:].reshape(req_dev, KV_HEADS, HEAD_DIM)
    token_score = (
        jnp.einsum("nkgd,nkd->nkg", grouped, token_keys, preferred_element_type=jnp.float32)
        * scale_factor
    )
    attention_all = (
        add_token(full_sum, full_max, full_total, token_score, token_values, "nkg,nkd->nkgd")
        .reshape(req_dev, HEADS * HEAD_DIM)
        .astype(jnp.bfloat16)
    )
    attention = lax.dynamic_slice_in_dim(attention_all, tp_index * slice_width, slice_width, 1)
    projected = jnp.dot(attention, w_output, preferred_element_type=jnp.float32)
    summed = lax.psum_scatter(
        projected.astype(jnp.bfloat16), "tp", scatter_dimension=1, tiled=True
    ).astype(jnp.float32)
    out_width = summed.shape[1]
    residual = lax.dynamic_slice_in_dim(hidden_in, tp_index * out_width, out_width, 1).astype(
        jnp.float32
    )
    hidden_out = (summed + residual).astype(jnp.bfloat16)
    return (hidden_out, new_keyval)


def solution(mesh):
    placed = (
        P("grp", None),
        P(),
        P(None, "tp"),
        P(None, "tp"),
        P("tp", None),
        P("grp", "tp", None),
        P("grp", "tp", None),
        P(),
        P(),
        P(),
        P("grp"),
    )
    return jax.shard_map(
        on_device,
        mesh=mesh,
        in_specs=placed,
        out_specs=(P("grp", "tp"), P("grp", "tp")),
        check_vma=False,
    )
```

profile of v0, /device:TPU:10, one launch (start us, length us, event | category | flops | bytes accessed | tf_op | source)
XLA Modules:
  0.0 476.1 jit_solution(16032584762213668495)
XLA Ops:
  16.5 30.2 %all_gather.23 = bf16[16,2048]{1,0:T(8,128)(2,1)} all-gather(bf16[16,256]{1,0:T(8,128)(2,1)S(1)} %convert_element_type.140), channel_id=1, replica_groups=mesh['grp'=32,'tp'=8] {'tp'}, dimensions={1}, use_global_device_ids=true | all-gather | bytes 73728 | tf_op jit(solution)/shard_map/all_gather | solution.py:144
  49.7 2.1 fusion.87
  51.8 2.1 fusion.88
  53.8 2.1 fusion.89
  55.9 41.3 %convert_reduce_fusion = (s32[]{:T(128)}, pred[512]{0:T(512)(128)(4,1)S(1)}, s32[512]{0:T(512)S(1)}) fusion(s32[512]{0:T(512)} %param.24, s32[]{:T(128)S(6)} %add.231, pred[]{:T(512)S(6)} %lt.150, s32[]{:T(128)} %bitcast.67, s32[]{:T(128)} %bitcast.66, s32[]{:T(128)} %bitcast.65, s32[]{:T(128)} %bitcast.64, s32[]{:T(128)} %bitcast.63, s32[]{:T(128)} %bitcast.62, ...), kind=kLoop, calls=%fused_computation.153 | loop fusion | flops 68607 | bytes 4873 | tf_op jit(solution)/shard_map/reduce_sum | solution.py:160
  98.6 3.8 top_k.17
  102.3 3.8 top_k.24
  110.2 4.3 gather_fusion.3
  116.4 2.0 copy.74
  129.9 2.1 fusion.16
  134.8 6.8 %scatter_fusion.4 = f32[512,2,32]{2,1,0:T(2,128)S(1)} fusion(f32[512,2,32]{2,1,0:T(2,128)S(1)} %broadcast.255.clone.1, s32[128]{0:T(128)S(1)} %fusion.77, f32[128,32]{1,0:T(8,128)S(1)} %copy.94), kind=kCustom, calls=%fused_computation.9 | custom fusion | flops 4096 | bytes 50176 | tf_op jit(solution)/shard_map/scatter-add | solution.py:181
  141.7 6.6 %scatter_fusion.2 = f32[512,2,32]{2,1,0:T(2,128)S(1)} fusion(f32[512,2,32]{2,1,0:T(2,128)S(1)} %broadcast.255.clone, s32[128]{0:T(128)S(1)} %fusion.77, f32[128,32]{1,0:T(8,128)S(1)} %copy.83), kind=kCustom, calls=%fused_computation.7 | custom fusion | flops 4096 | bytes 50176 | tf_op jit(solution)/shard_map/scatter-add | solution.py:178
  148.3 6.6 %scatter_fusion.5 = f32[512,2,32]{2,1,0:T(2,128)S(1)} fusion(f32[512,2,32]{2,1,0:T(2,128)S(1)} %scatter_fusion.4, s32[128]{0:T(128)S(1)} %fusion.78, f32[128,32]{1,0:T(8,128)S(1)} %copy.95), kind=kCustom, calls=%fused_computation.10 | custom fusion | flops 4096 | bytes 50176 | tf_op jit(solution)/shard_map/scatter-add | solution.py:181
  154.9 6.6 %scatter_fusion.3 = f32[512,2,32]{2,1,0:T(2,128)S(1)} fusion(f32[512,2,32]{2,1,0:T(2,128)S(1)} %scatter_fusion.2, s32[128]{0:T(128)S(1)} %fusion.78, f32[128,32]{1,0:T(8,128)S(1)} %copy.84), kind=kCustom, calls=%fused_computation.8 | custom fusion | flops 4096 | bytes 50176 | tf_op jit(solution)/shard_map/scatter-add | solution.py:178
  161.5 7.5 %broadcast_in_dim.180 = f32[512,2,2048]{2,1,0:T(2,128)} broadcast(f32[]{:T(128)} %constant.85.clone.1), dimensions={} | broadcast | bytes 8388612 | tf_op jit(solution)/shard_map/broadcast_in_dim | solution.py:169
  169.0 21.2 %scatter_fusion = f32[512,2,2048]{2,1,0:T(2,128)} fusion(f32[512,2,2048]{2,1,0:T(2,128)} %broadcast_in_dim.180, s32[128]{0:T(128)S(1)} %fusion.77, f32[128,2048]{1,0:T(8,128)S(1)} %broadcast_select_fusion.1), kind=kCustom, calls=%fused_computation.5 | custom fusion | flops 262144 | bytes 3146752 | tf_op jit(solution)/shard_map/scatter-add | solution.py:175
  190.3 22.7 %scatter_fusion.1 = f32[512,2,2048]{2,1,0:T(2,128)} fusion(f32[512,2,2048]{2,1,0:T(2,128)} %scatter_fusion, s32[128]{0:T(128)S(1)} %fusion.78, f32[128,2048]{1,0:T(8,128)} %broadcast_select_fusion), kind=kCustom, calls=%fused_computation.6 | custom fusion | flops 262144 | bytes 3146752 | tf_op jit(solution)/shard_map/scatter-add | solution.py:175
  218.5 24.5 %all-gather.1 = bf16[8,64,16]{1,2,0:T(8,128)(2,1)S(1)} all-gather(bf16[1,64,16]{1,2,0:T(8,128)(2,1)S(1)} %bitcast.283), channel_id=1, replica_groups=mesh['grp'=32,'tp'=8] {'tp'}, dimensions={0}, use_global_device_ids=true | all-gather | bytes 18432 | tf_op jit(solution)/shard_map/all_gather | solution.py:145
  244.7 99.7 %all-reduce.8.cloned.1.call-done = (f32[512,2,2048]{2,1,0:T(2,128)}, f32[512,2,32]{2,1,0:T(2,128)}, f32[512,2,32]{2,1,0:T(2,128)}) async-done(((f32[512,2,2048]{2,1,0:T(2,128)}, f32[512,2,32]{2,1,0:T(2,128)}, f32[512,2,32]{2,1,0:T(2,128)}), (f32[512,2,2048]{2,1,0:T(2,128)}, f32[512,2,32]{2,1,0:T(2,128)}, f32[512,2,32]{2,1,0:T(2,128)})) %all-reduce.8.cloned.1.call-update) | async-done | bytes 8650768
  346.6 26.0 %all_gather.28 = bf16[8,16,4,8]{1,3,2,0:T(8,128)(2,1)S(1)} all-gather(bf16[1,16,4,8]{1,3,2,0:T(8,128)(2,1)S(1)} %fusion.49), channel_id=1, replica_groups=mesh['grp'=32,'tp'=8] {'tp'}, dimensions={0}, use_global_device_ids=true | all-gather | bytes 9216 | tf_op jit(solution)/shard_map/all_gather | solution.py:15
  376.1 26.8 %all-gather = bf16[128,4,8,64]{3,2,1,0:T(8,128)(2,1)S(1)} all-gather(bf16[16,4,8,64]{3,2,1,0:T(8,128)(2,1)S(1)} %fusion.9), channel_id=2, replica_groups=mesh['grp'=32,'tp'=8] {'tp'}, dimensions={0}, use_global_device_ids=true | all-gather | bytes 589824 | tf_op jit(solution)/shard_map/all_gather | solution.py:15
  402.9 24.6 %all_gather.27 = bf16[8,16,4,8]{1,3,2,0:T(8,128)(2,1)S(1)} all-gather(bf16[1,16,4,8]{1,3,2,0:T(8,128)(2,1)S(1)} %fusion.56), channel_id=1, replica_groups=mesh['grp'=32,'tp'=8] {'tp'}, dimensions={0}, use_global_device_ids=true | all-gather | bytes 9216 | tf_op jit(solution)/shard_map/all_gather | solution.py:15
  427.5 3.9 while.19
  432.9 35.4 %reduce-scatter.2.cloned.1.call-done = bf16[16,256]{1,0:T(8,128)(2,1)} async-done(((bf16[16,2048]{1,0:T(8,128)(2,1)}), bf16[16,256]{1,0:T(8,128)(2,1)}) %reduce-scatter.2.cloned.1.call-update) | async-done | bytes 8208 | tf_op jit(solution)/shard_map/reduce_scatter | solution.py:213
  (199 shorter events, 52.2 us)
Async XLA Ops:
  7.2 424.8 %copy-start = (bf16[256,2048]{1,0:T(8,128)(2,1)S(1)}, bf16[256,2048]{1,0:T(8,128)(2,1)}, u32[]{:S(2)}) copy-start(bf16[256,2048]{1,0:T(8,128)(2,1)} %param.19) | copy-start | bytes 3145732
  7.2 103.0 %all-gather.4.cloned.1.call-start = ((), (), s32[]{:S(2)}) async-start(), calls=%async_computation.1 | async-start | bytes 2162688 | tf_op jit(solution)/shard_map/all_gather | solution.py:147
  7.2 102.9 %copy-start.18 = (f32[32]{0:T(128)}, f32[32]{0:T(128)S(1)}, u32[]{:S(2)}) copy-start(f32[32]{0:T(128)S(1)} %multiply_exponential_fusion) | copy-start | bytes 388
  13.7 1.6 copy-start.21
  16.1 94.1 %copy-start.13 = (f32[16]{0:T(128)}, f32[16]{0:T(128)S(1)}, u32[]{:S(2)}) copy-start(f32[16]{0:T(128)S(1)} %add_convert_fusion.2) | copy-start | bytes 196
  46.7 297.8 %all-reduce.8.cloned.1.call-start = ((), (), s32[]{:S(2)}) async-start(), calls=%async_computation.3 | async-start | bytes 18874368
  108.1 16.5 %copy-start.17 = (pred[128]{0:T(512)(128)(4,1)}, pred[128]{0:T(512)(128)(4,1)S(1)}, u32[]{:S(2)}) copy-start(pred[128]{0:T(512)(128)(4,1)S(1)} %iota_compare_fusion.1) | copy-start | bytes 388
  108.8 16.2 %copy-start.15 = (pred[128]{0:T(512)(128)(4,1)}, pred[128]{0:T(512)(128)(4,1)S(1)}, u32[]{:S(2)}) copy-start(pred[128]{0:T(512)(128)(4,1)S(1)} %iota_compare_fusion) | copy-start | bytes 388
  110.0 9.8 %copy-start.12 = (pred[64]{0:T(512)(128)(4,1)}, pred[64]{0:T(512)(128)(4,1)S(1)}, u32[]{:S(2)}) copy-start(pred[64]{0:T(512)(128)(4,1)S(1)} %get-tuple-element.351) | copy-start | bytes 196
  110.0 14.6 %copy-start.11 = (pred[64]{0:T(512)(128)(4,1)}, pred[64]{0:T(512)(128)(4,1)S(1)}, u32[]{:S(2)}) copy-start(pred[64]{0:T(512)(128)(4,1)S(1)} %get-tuple-element.350) | copy-start | bytes 196
  110.2 11.0 %copy-start.1 = (bf16[512,2048]{1,0:T(8,128)(2,1)S(1)}, bf16[512,2048]{1,0:T(8,128)(2,1)}, u32[]{:S(2)}) copy-start(bf16[512,2048]{1,0:T(8,128)(2,1)} %all-gather.4.cloned.1.call-done) | copy-start | bytes 6291460
  119.8 1.2 copy-start.8
  127.2 6.3 %copy-start.16 = (pred[128]{0:T(512)(128)(4,1)S(1)}, pred[128]{0:T(512)(128)(4,1)}, u32[]{:S(2)}) copy-start(pred[128]{0:T(512)(128)(4,1)} %copy-done.15) | copy-start | bytes 388
  154.9 35.3 %copy-start.3 = (f32[512,2,32]{2,1,0:T(2,128)}, f32[512,2,32]{2,1,0:T(2,128)S(1)}, u32[]{:S(2)}) copy-start(f32[512,2,32]{2,1,0:T(2,128)S(1)} %scatter_fusion.5) | copy-start | bytes 393220
  161.5 28.7 %copy-start.4 = (f32[512,2,32]{2,1,0:T(2,128)}, f32[512,2,32]{2,1,0:T(2,128)S(1)}, u32[]{:S(2)}) copy-start(f32[512,2,32]{2,1,0:T(2,128)S(1)} %scatter_fusion.3) | copy-start | bytes 393220
  213.0 1.3 copy-start.5
  213.0 1.8 copy-start.20
  213.0 4.2 copy-start.7
  213.0 4.2 copy-start.22
  213.0 5.3 %copy-start.14 = (f32[16]{0:T(128)S(1)}, f32[16]{0:T(128)}, u32[]{:S(2)}) copy-start(f32[16]{0:T(128)} %copy-done.13) | copy-start | bytes 196
  213.0 5.3 %copy-start.19 = (f32[32]{0:T(128)S(1)}, f32[32]{0:T(128)}, u32[]{:S(2)}) copy-start(f32[32]{0:T(128)} %copy-done.18) | copy-start | bytes 388
  213.0 30.3 %copy-start.23 = (u32[256]{0:T(256)S(1)}, u32[256]{0:T(256)}, u32[]{:S(2)}) copy-start(u32[256]{0:T(256)} %constant.274) | copy-start | bytes 3076
  213.1 255.2 %reduce-scatter.2.cloned.1.call-start = ((), (), s32[]{:S(2)}) async-start(), calls=%async_computation.2 | async-start | bytes 73728 | tf_op jit(solution)/shard_map/reduce_scatter | solution.py:213
  218.5 214.3 %copy-start.10 = (bf16[16,64]{1,0:T(8,128)(2,1)}, bf16[16,64]{1,0:T(8,128)(2,1)S(1)}, u32[]{:S(2)}) copy-start(bf16[16,64]{1,0:T(8,128)(2,1)S(1)} %fusion.71) | copy-start | bytes 6148
  (3 other events, 2.4 us)
Sparse Core Ops, SparseCore 0:
  46.8 46.4 all-gather.3
  213.2 131.2 all-reduce.7
  433.0 35.2 reduce-scatter.1
where the time goes:
time: 478 us; the launch traced here: 476 us
  other arithmetic  137 us (29%)
  waiting for transfers between devices  135 us (28%)
  blocking collectives  132 us (28%)
  local copies, waits for them, and re-layouts  44.5 us (9%)
  between operations  15.1 us (3%)
  matrix products  11.6 us (2%)
    unnamed x4, waiting for transfers between devices  99.7 us
    all_gather x3, blocking collectives, combined_all(): lax.all_gather(part.astype(kind), axis)  77.3 us
    scatter-add x2, other arithmetic, on_device(): sum_rows.at[picked, level_slot]  43.9 us
    reduce_sum x2, other arithmetic, on_device(): filled = jnp.arange(per_tenant) < jnp.sum(member.astype(jnp.int32))  42.6 us
    reduce_scatter x1, waiting for transfers between devices, on_device(): lax.psum_scatter(projected.astype(jnp.bfloat16), 'tp', scatter_dimension=...  35.4 us
    all_gather x1, blocking collectives, on_device(): lax.all_gather(query_rot, 'tp', axis=1, tiled=True)  30.2 us
    all_gather x1, blocking collectives, on_device(): lax.all_gather(new_keyval, 'tp', axis=1, tiled=True)  24.5 us
    scatter-add x2, other arithmetic, on_device(): total_rows.at[picked, level_slot]  13.4 us
  transfers between devices with their start and end apart: 3, of which 2 were waited for; matrix products, arithmetic and copies ran while one was open for 14% of the time, Pallas kernels for 0%

commit v1 on v0

--- a/solution.py
+++ b/solution.py
@@ -141,7 +141,9 @@
         .astype(jnp.bfloat16)
     )
     query_all, keyval_all = (
-        lax.all_gather(query_rot, "tp", axis=1, tiled=True),
+        jnp.concatenate(
+            lax.all_to_all(jnp.stack([query_rot] * lax.axis_size("tp")), "tp", 0, 0), 1
+        ),
         lax.all_gather(new_keyval, "tp", axis=1, tiled=True),
     )
     everyone = lax.all_gather(query_all, "grp", axis=0, tiled=True)

time: 478 us -> 464 us (0.971)
  blocking collectives: 132 us -> 118 us
    all_gather x1 -> x0, blocking collectives: 30.2 us -> none  [on_device(): lax.all_gather(query_rot, 'tp', axis=1, tiled=True)]
    all_to_all x0 -> x1, blocking collectives: none -> 16.6 us  [on_device(): lax.all_to_all(jnp.stack([query_rot] * lax.axis_size('tp')), 'tp', 0, 0)]
  transfers between devices with their start and end apart: 3 -> 3, of which waited for: 2 -> 2; matrix products, arithmetic and copies ran while one was open for 14% -> 15% of each run, Pallas kernels for 0% -> 0%
where the time goes in v1:
time: 464 us; the launch traced here: 462 us
  other arithmetic  138 us (30%)
  waiting for transfers between devices  132 us (28%)
  blocking collectives  118 us (25%)
  local copies, waits for them, and re-layouts  45.8 us (10%)
  between operations  15.1 us (3%)
  matrix products  11.5 us (2%)
    unnamed x4, waiting for transfers between devices  96.7 us
    all_gather x3, blocking collectives, combined_all(): lax.all_gather(part.astype(kind), axis)  77.3 us
    scatter-add x2, other arithmetic, on_device(): sum_rows.at[picked, level_slot]  43.9 us
    reduce_sum x2, other arithmetic, on_device(): filled = jnp.arange(per_tenant) < jnp.sum(member.astype(jnp.int32))  42.8 us
    reduce_scatter x1, waiting for transfers between devices, on_device(): lax.psum_scatter(projected.astype(jnp.bfloat16), 'tp', scatter_dimension=...  35.4 us
    all_gather x1, blocking collectives, on_device(): lax.all_gather(new_keyval, 'tp', axis=1, tiled=True)  24.5 us
    all_to_all x1, blocking collectives, on_device(): lax.all_to_all(jnp.stack([query_rot] * lax.axis_size('tp')), 'tp', 0, 0)  16.6 us
    scatter-add x2, other arithmetic, on_device(): total_rows.at[picked, level_slot]  13.4 us
  transfers between devices with their start and end apart: 3, of which 2 were waited for; matrix products, arithmetic and copies ran while one was open for 15% of the time, Pallas kernels for 0%

profile of v1, /device:TPU:10, one launch (start us, length us, event | category | flops | bytes accessed | tf_op | source)
XLA Modules:
  0.0 461.5 jit_solution(16765370477193713853)
XLA Ops:
  16.5 16.6 %all_to_all.5 = bf16[8,16,256]{2,1,0:T(8,128)(2,1)S(1)} all-to-all(bf16[8,16,256]{2,1,0:T(8,128)(2,1)S(1)} %stack.2), channel_id=1, replica_groups=mesh['grp'=32,'tp'=8] {'tp'}, dimensions={0} | all-to-all | bytes 131072 | tf_op jit(solution)/shard_map/all_to_all | solution.py:145
  37.4 2.1 fusion.87
  39.5 2.1 fusion.88
  41.5 2.1 fusion.89
  43.6 41.5 %convert_reduce_fusion = (s32[]{:T(128)}, pred[512]{0:T(512)(128)(4,1)S(1)}, s32[512]{0:T(512)S(1)}) fusion(s32[512]{0:T(512)} %param.24, s32[]{:T(128)S(6)} %add.231, pred[]{:T(512)S(6)} %lt.150, s32[]{:T(128)} %bitcast.67, s32[]{:T(128)} %bitcast.66, s32[]{:T(128)} %bitcast.65, s32[]{:T(128)} %bitcast.64, s32[]{:T(128)} %bitcast.63, s32[]{:T(128)} %bitcast.62, ...), kind=kLoop, calls=%fused_computation.153 | loop fusion | flops 68607 | bytes 4873 | tf_op jit(solution)/shard_map/reduce_sum | solution.py:162
  86.5 3.8 top_k.17
  90.3 3.8 top_k.24
  98.0 4.3 gather_fusion.3
  104.2 2.0 copy.77
  117.7 2.1 fusion.16
  123.2 6.8 %scatter_fusion.4 = f32[512,2,32]{2,1,0:T(2,128)S(1)} fusion(f32[512,2,32]{2,1,0:T(2,128)S(1)} %broadcast.256.clone.1, s32[128]{0:T(128)S(1)} %fusion.77, f32[128,32]{1,0:T(8,128)S(1)} %copy.98), kind=kCustom, calls=%fused_computation.9 | custom fusion | flops 4096 | bytes 50176 | tf_op jit(solution)/shard_map/scatter-add | solution.py:183
  130.2 6.6 %scatter_fusion.2 = f32[512,2,32]{2,1,0:T(2,128)S(1)} fusion(f32[512,2,32]{2,1,0:T(2,128)S(1)} %broadcast.256.clone, s32[128]{0:T(128)S(1)} %fusion.77, f32[128,32]{1,0:T(8,128)S(1)} %copy.86), kind=kCustom, calls=%fused_computation.7 | custom fusion | flops 4096 | bytes 50176 | tf_op jit(solution)/shard_map/scatter-add | solution.py:180
  136.8 6.6 %scatter_fusion.5 = f32[512,2,32]{2,1,0:T(2,128)S(1)} fusion(f32[512,2,32]{2,1,0:T(2,128)S(1)} %scatter_fusion.4, s32[128]{0:T(128)S(1)} %fusion.78, f32[128,32]{1,0:T(8,128)S(1)} %copy.99), kind=kCustom, calls=%fused_computation.10 | custom fusion | flops 4096 | bytes 50176 | tf_op jit(solution)/shard_map/scatter-add | solution.py:183
  143.4 6.6 %scatter_fusion.3 = f32[512,2,32]{2,1,0:T(2,128)S(1)} fusion(f32[512,2,32]{2,1,0:T(2,128)S(1)} %scatter_fusion.2, s32[128]{0:T(128)S(1)} %fusion.78, f32[128,32]{1,0:T(8,128)S(1)} %copy.87), kind=kCustom, calls=%fused_computation.8 | custom fusion | flops 4096 | bytes 50176 | tf_op jit(solution)/shard_map/scatter-add | solution.py:180
  150.0 7.5 %broadcast_in_dim.180 = f32[512,2,2048]{2,1,0:T(2,128)} broadcast(f32[]{:T(128)} %constant.85.clone.1), dimensions={} | broadcast | bytes 8388612 | tf_op jit(solution)/shard_map/broadcast_in_dim | solution.py:171
  157.5 21.2 %scatter_fusion = f32[512,2,2048]{2,1,0:T(2,128)} fusion(f32[512,2,2048]{2,1,0:T(2,128)} %broadcast_in_dim.180, s32[128]{0:T(128)S(1)} %fusion.77, f32[128,2048]{1,0:T(8,128)S(1)} %broadcast_select_fusion.1), kind=kCustom, calls=%fused_computation.5 | custom fusion | flops 262144 | bytes 3146752 | tf_op jit(solution)/shard_map/scatter-add | solution.py:177
  178.7 22.7 %scatter_fusion.1 = f32[512,2,2048]{2,1,0:T(2,128)} fusion(f32[512,2,2048]{2,1,0:T(2,128)} %scatter_fusion, s32[128]{0:T(128)S(1)} %fusion.78, f32[128,2048]{1,0:T(8,128)} %broadcast_select_fusion), kind=kCustom, calls=%fused_computation.6 | custom fusion | flops 262144 | bytes 3146752 | tf_op jit(solution)/shard_map/scatter-add | solution.py:177
  206.0 24.5 %all-gather.1 = bf16[8,64,16]{1,2,0:T(8,128)(2,1)S(1)} all-gather(bf16[1,64,16]{1,2,0:T(8,128)(2,1)S(1)} %bitcast.289), channel_id=1, replica_groups=mesh['grp'=32,'tp'=8] {'tp'}, dimensions={0}, use_global_device_ids=true | all-gather | bytes 18432 | tf_op jit(solution)/shard_map/all_gather | solution.py:147
  233.3 96.6 %all-reduce.8.cloned.1.call-done = (f32[512,2,2048]{2,1,0:T(2,128)}, f32[512,2,32]{2,1,0:T(2,128)}, f32[512,2,32]{2,1,0:T(2,128)}) async-done(((f32[512,2,2048]{2,1,0:T(2,128)}, f32[512,2,32]{2,1,0:T(2,128)}, f32[512,2,32]{2,1,0:T(2,128)}), (f32[512,2,2048]{2,1,0:T(2,128)}, f32[512,2,32]{2,1,0:T(2,128)}, f32[512,2,32]{2,1,0:T(2,128)})) %all-reduce.8.cloned.1.call-update) | async-done | bytes 8650768
  332.0 26.0 %all_gather.24 = bf16[8,16,4,8]{1,3,2,0:T(8,128)(2,1)S(1)} all-gather(bf16[1,16,4,8]{1,3,2,0:T(8,128)(2,1)S(1)} %fusion.49), channel_id=1, replica_groups=mesh['grp'=32,'tp'=8] {'tp'}, dimensions={0}, use_global_device_ids=true | all-gather | bytes 9216 | tf_op jit(solution)/shard_map/all_gather | solution.py:15
  361.5 26.8 %all-gather = bf16[128,4,8,64]{3,2,1,0:T(8,128)(2,1)S(1)} all-gather(bf16[16,4,8,64]{3,2,1,0:T(8,128)(2,1)S(1)} %fusion.9), channel_id=2, replica_groups=mesh['grp'=32,'tp'=8] {'tp'}, dimensions={0}, use_global_device_ids=true | all-gather | bytes 589824 | tf_op jit(solution)/shard_map/all_gather | solution.py:15
  388.3 24.6 %all_gather.23 = bf16[8,16,4,8]{1,3,2,0:T(8,128)(2,1)S(1)} all-gather(bf16[1,16,4,8]{1,3,2,0:T(8,128)(2,1)S(1)} %fusion.56), channel_id=1, replica_groups=mesh['grp'=32,'tp'=8] {'tp'}, dimensions={0}, use_global_device_ids=true | all-gather | bytes 9216 | tf_op jit(solution)/shard_map/all_gather | solution.py:15
  413.0 3.9 while.19
  418.3 35.4 %reduce-scatter.2.cloned.1.call-done = bf16[16,256]{1,0:T(8,128)(2,1)} async-done(((bf16[16,2048]{1,0:T(8,128)(2,1)}), bf16[16,256]{1,0:T(8,128)(2,1)}) %reduce-scatter.2.cloned.1.call-update) | async-done | bytes 8208 | tf_op jit(solution)/shard_map/reduce_scatter | solution.py:215
  (198 shorter events, 54.1 us)
Async XLA Ops:
  7.2 410.3 %copy-start = (bf16[256,2048]{1,0:T(8,128)(2,1)S(1)}, bf16[256,2048]{1,0:T(8,128)(2,1)}, u32[]{:S(2)}) copy-start(bf16[256,2048]{1,0:T(8,128)(2,1)} %param.19) | copy-start | bytes 3145732
  7.2 90.8 %all-gather.4.cloned.1.call-start = ((), (), s32[]{:S(2)}) async-start(), calls=%async_computation.2 | async-start | bytes 2162688 | tf_op jit(solution)/shard_map/all_gather | solution.py:149
  7.2 27.5 %copy-start.16 = (f32[32]{0:T(128)}, f32[32]{0:T(128)S(1)}, u32[]{:S(2)}) copy-start(f32[32]{0:T(128)S(1)} %multiply_exponential_fusion) | copy-start | bytes 388
  13.7 1.6 copy-start.19
  16.1 18.7 %copy-start.12 = (f32[16]{0:T(128)}, f32[16]{0:T(128)S(1)}, u32[]{:S(2)}) copy-start(f32[16]{0:T(128)S(1)} %add_convert_fusion.2) | copy-start | bytes 196
  33.8 296.1 %all-reduce.8.cloned.1.call-start = ((), (), s32[]{:S(2)}) async-start(), calls=%async_computation.4 | async-start | bytes 18874368
  96.0 16.5 %copy-start.15 = (pred[128]{0:T(512)(128)(4,1)}, pred[128]{0:T(512)(128)(4,1)S(1)}, u32[]{:S(2)}) copy-start(pred[128]{0:T(512)(128)(4,1)S(1)} %iota_compare_fusion.1) | copy-start | bytes 388
  96.6 16.1 %copy-start.14 = (pred[128]{0:T(512)(128)(4,1)}, pred[128]{0:T(512)(128)(4,1)S(1)}, u32[]{:S(2)}) copy-start(pred[128]{0:T(512)(128)(4,1)S(1)} %iota_compare_fusion) | copy-start | bytes 388
  97.9 9.8 %copy-start.11 = (pred[64]{0:T(512)(128)(4,1)}, pred[64]{0:T(512)(128)(4,1)S(1)}, u32[]{:S(2)}) copy-start(pred[64]{0:T(512)(128)(4,1)S(1)} %get-tuple-element.351) | copy-start | bytes 196
  97.9 14.6 %copy-start.10 = (pred[64]{0:T(512)(128)(4,1)}, pred[64]{0:T(512)(128)(4,1)S(1)}, u32[]{:S(2)}) copy-start(pred[64]{0:T(512)(128)(4,1)S(1)} %get-tuple-element.350) | copy-start | bytes 196
  98.0 11.0 %copy-start.1 = (bf16[512,2048]{1,0:T(8,128)(2,1)S(1)}, bf16[512,2048]{1,0:T(8,128)(2,1)}, u32[]{:S(2)}) copy-start(bf16[512,2048]{1,0:T(8,128)(2,1)} %all-gather.4.cloned.1.call-done) | copy-start | bytes 6291460
  107.6 1.0 copy-start.2
  107.6 1.2 copy-start.7
  143.4 35.3 %copy-start.3 = (f32[512,2,32]{2,1,0:T(2,128)}, f32[512,2,32]{2,1,0:T(2,128)S(1)}, u32[]{:S(2)}) copy-start(f32[512,2,32]{2,1,0:T(2,128)S(1)} %scatter_fusion.5) | copy-start | bytes 393220
  150.0 28.7 %copy-start.4 = (f32[512,2,32]{2,1,0:T(2,128)}, f32[512,2,32]{2,1,0:T(2,128)S(1)}, u32[]{:S(2)}) copy-start(f32[512,2,32]{2,1,0:T(2,128)S(1)} %scatter_fusion.3) | copy-start | bytes 393220
  201.4 1.2 copy-start.5
  201.4 3.2 copy-start.6
  201.4 3.2 copy-start.20
  201.4 4.4 copy-start.13
  201.4 4.4 copy-start.17
  201.4 29.3 %copy-start.21 = (u32[256]{0:T(256)S(1)}, u32[256]{0:T(256)}, u32[]{:S(2)}) copy-start(u32[256]{0:T(256)} %constant.274) | copy-start | bytes 3076
  201.4 30.6 %copy-start.18 = (s32[16]{0:T(128)S(1)}, s32[16]{0:T(128)}, u32[]{:S(2)}) copy-start(s32[16]{0:T(128)} %param.25) | copy-start | bytes 196
  201.5 252.2 %reduce-scatter.2.cloned.1.call-start = ((), (), s32[]{:S(2)}) async-start(), calls=%async_computation.3 | async-start | bytes 73728 | tf_op jit(solution)/shard_map/reduce_scatter | solution.py:215
  206.0 207.0 %copy-start.9 = (bf16[16,64]{1,0:T(8,128)(2,1)}, bf16[16,64]{1,0:T(8,128)(2,1)S(1)}, u32[]{:S(2)}) copy-start(bf16[16,64]{1,0:T(8,128)(2,1)S(1)} %fusion.71) | copy-start | bytes 6148
  (1 other events, 0.6 us)
Sparse Core Ops, SparseCore 0:
  33.9 43.4 all-gather.3
  201.6 128.2 all-reduce.7
  418.5 35.2 reduce-scatter.1
